TPU v7x, 512 devices: a whole 4x4x16 slice. The times are simulated.
512 devices in a mesh: band: 128 (over z, y, x_lo), domain: 4 (over x_hi, core).
Axes of the slice: x: 4 (x_hi: 2, x_lo: 2; x = x_hi * 2 + x_lo), y: 4, z: 16, core: 2. Of those that a mesh axis runs over, the one named last changes fastest.
Arguments:
- orbitals: bfloat16 [1024, 8, 5120], P('band', 'domain'), may hold values from -6 to 6
- boundary: bfloat16 [1024, 4, 5120], P('band'), may hold values from -6 to 6
- potential: bfloat16 [8, 5120], P('domain'), may hold values from 0 to 2
Outputs:
- correlation: float32 [1024, 1024], P('band', 'domain')
- projected: float32 [1024, 1024], P('band', 'domain')
All inputs are finite; a program needn't handle non-finite values.
Results may differ from a plain program's by a relative error of at most 0.0012.
Values may be sent and summed in bfloat16 or wider, within the bound.
No kernel may reach another device: no remote copies, remote signals or barrier semaphores. Data moves between devices by JAX's collectives and lax.ppermute only.
A program may use at most 128 MiB of HBM per device.

v0:
```python
import jax
import jax.numpy as jnp
from jax import lax
from jax.sharding import PartitionSpec as P

NX = 160
NY = 32
NZ_DEV = 2
DEGREE = 4
filter_center = 5.5
filter_radius = 4.5


def padded_2(cells, sides, width):
    for axis, dim in sides:
        count = lax.axis_size(axis)
        ends = count - 1
        head = lax.slice_in_dim(cells, 0, width, axis=dim)
        tail = lax.slice_in_dim(cells, cells.shape[dim] - width, cells.shape[dim], axis=dim)
        cells = jnp.concatenate(
            [
                lax.ppermute(tail, axis, [(i, (i + 1) % count) for i in range(ends)]),
                cells,
                lax.ppermute(head, axis, [((i + 1) % count, i) for i in range(ends)]),
            ],
            axis=dim,
        )
    return cells


def second_diff(values, axis_pos):
    near = jnp.roll(values, 1, axis_pos) + jnp.roll(values, -1, axis_pos)
    far = jnp.roll(values, 2, axis_pos) + jnp.roll(values, -2, axis_pos)
    return (16.0 * near - far - 30.0 * values) / 12.0


def plane_part(values):
    shaped = values.reshape(values.shape[:-1] + (NY, NX))
    total = second_diff(shaped, -1) + second_diff(shaped, -2)
    return total.reshape(values.shape)


def hamiltonian(padded, potential):
    middle = padded[:, 2:-2]
    z_part = (
        16.0 * (padded[:, 1:-3] + padded[:, 3:-1])
        - (padded[:, :-4] + padded[:, 4:])
        - 30.0 * middle
    ) / 12.0
    laplace = z_part + plane_part(middle)
    return -0.5 * laplace + potential.astype(jnp.float32) * middle


def chebyshev(apply_ham, orb_block):
    earlier = orb_block
    current = (
        (apply_ham(orb_block) - filter_center * orb_block.astype(jnp.float32)) / filter_radius
    ).astype(jnp.bfloat16)
    for degree_step in range(DEGREE - 1):
        following = (
            2.0 * (apply_ham(current) - filter_center * current.astype(jnp.float32)) / filter_radius
        )
        following = (following - earlier.astype(jnp.float32)).astype(jnp.bfloat16)
        earlier, current = (current, following)
    return (current, apply_ham(current).astype(jnp.bfloat16))


def per_device(orbitals, boundary, potential):
    orb_count = orbitals.shape[0]
    domain_pos = lax.axis_index("domain")
    domain_count = lax.axis_size("domain")
    last_pos = domain_count - 1

    def apply_ham(values):
        padded = padded_2(values, (("domain", 1),), 2)
        lower_rim = jnp.where(domain_pos == 0, boundary[:, 0:2], padded[:, 0:2])
        upper_rim = jnp.where(domain_pos == last_pos, boundary[:, 2:4], padded[:, -2:])
        padded = jnp.concatenate([lower_rim, padded[:, 2:-2], upper_rim], axis=1).astype(
            jnp.float32
        )
        return hamiltonian(padded, potential)

    filtered, applied = chebyshev(apply_ham, orbitals)
    filtered = filtered.reshape(orb_count, -1)
    applied = applied.reshape(orb_count, -1)
    cell_y, cell_h = (
        lax.all_to_all(filtered, "band", split_axis=1, concat_axis=0, tiled=True),
        lax.all_to_all(applied, "band", split_axis=1, concat_axis=0, tiled=True),
    )
    cell_y, cell_h = (
        lax.all_gather(cell_y, "domain", axis=1, tiled=True),
        lax.all_gather(cell_h, "domain", axis=1, tiled=True),
    )
    column_count = cell_y.shape[0] // domain_count
    column_y = lax.dynamic_slice_in_dim(cell_y, domain_pos * column_count, column_count, 0)
    column_h = lax.dynamic_slice_in_dim(cell_h, domain_pos * column_count, column_count, 0)
    contract_dims = (((1,), (1,)), ((), ()))
    with_y = lax.dot_general(cell_y, column_y, contract_dims, preferred_element_type=jnp.float32)
    with_h = lax.dot_general(cell_y, column_h, contract_dims, preferred_element_type=jnp.float32)
    summed = lax.psum_scatter(
        jnp.concatenate([with_y, with_h], axis=1), "band", scatter_dimension=0, tiled=True
    )
    total_cells = NZ_DEV * NY * NX * domain_count
    correlation = summed[:, :column_count] / total_cells
    projected = summed[:, column_count:] / total_cells
    return (correlation, projected)


def solution(mesh):
    return jax.shard_map(
        per_device,
        mesh=mesh,
        in_specs=(P("band", "domain", None), P("band", None, None), P("domain", None)),
        out_specs=(P("band", "domain"), P("band", "domain")),
        check_vma=False,
    )
```

profile of v0, /device:TPU:4, one launch (start us, length us, event | category | flops | bytes accessed | tf_op | source)
XLA Modules:
  0.0 797.5 jit_solution(4684403561107533573)
XLA Ops:
  8.1 1.9 collective-permute-start.1
  10.0 2.4 collective-permute-start
  14.7 6.3 collective-permute-done
  29.2 1.9 collective-permute-start.3
  31.1 2.4 collective-permute-start.2
  34.0 5.3 collective-permute-done.2
  44.4 2.0 fusion.5
  47.9 1.9 collective-permute-start.5
  49.9 2.4 collective-permute-start.4
  52.7 5.3 collective-permute-done.4
  63.2 2.0 fusion.9
  66.6 1.9 collective-permute-start.7
  68.5 2.6 collective-permute-start.6
  71.4 5.3 collective-permute-done.6
  81.8 2.0 fusion.13
  85.3 1.9 collective-permute-start.9
  87.4 2.4 collective-permute-start.8
  91.0 19.2 %all-to-all-start = ((bf16[8,128,80]{2,0,1:T(8,128)(2,1)}), bf16[8,128,80]{2,0,1:T(8,128)(2,1)}, u32[]{:S(2)}, u32[]{:S(2)}) async-start(bf16[8,128,80]{2,0,1:T(8,128)(2,1)} %copy.26), calls=%async_computation | async-start | bytes 524288 | tf_op jit(solution)/shard_map/all_to_all | solution.py:87
  118.1 11.0 %all-to-all-done = bf16[8,128,80]{2,0,1:T(8,128)(2,1)} async-done(((bf16[8,128,80]{2,0,1:T(8,128)(2,1)}), bf16[8,128,80]{2,0,1:T(8,128)(2,1)}, u32[]{:S(2)}, u32[]{:S(2)}) %all-to-all-start) | async-done | bytes 163872 | tf_op jit(solution)/shard_map/all_to_all | solution.py:87
  129.1 9.1 %all-to-all-start.1 = ((bf16[8,128,80]{2,0,1:T(8,128)(2,1)}), bf16[8,128,80]{2,0,1:T(8,128)(2,1)S(1)}, u32[]{:S(2)}, u32[]{:S(2)}) async-start(bf16[8,128,80]{2,0,1:T(8,128)(2,1)} %copy.29), calls=%async_computation.1 | async-start | bytes 524288 | tf_op jit(solution)/shard_map/all_to_all | solution.py:88
  139.3 9.0 %all_gather.6 = bf16[1024,320]{0,1:T(8,128)(2,1)S(1)} all-gather(bf16[1024,80]{0,1:T(8,128)(2,1)S(1)} %copy.27), channel_id=1, replica_groups=mesh['band'=128,'domain'=4] {'domain'}, dimensions={1}, use_global_device_ids=true | all-gather | bytes 819200 | tf_op jit(solution)/shard_map/all_gather | solution.py:91
  148.9 8.1 %all-to-all-done.1 = bf16[8,128,80]{2,0,1:T(8,128)(2,1)S(1)} async-done(((bf16[8,128,80]{2,0,1:T(8,128)(2,1)}), bf16[8,128,80]{2,0,1:T(8,128)(2,1)S(1)}, u32[]{:S(2)}, u32[]{:S(2)}) %all-to-all-start.1) | async-done | bytes 163872 | tf_op jit(solution)/shard_map/all_to_all | solution.py:88
  157.1 8.4 %all_gather.7 = bf16[1024,320]{0,1:T(8,128)(2,1)S(1)} all-gather(bf16[1024,80]{0,1:T(8,128)(2,1)S(1)} %copy.30), channel_id=1, replica_groups=mesh['band'=128,'domain'=4] {'domain'}, dimensions={1}, use_global_device_ids=true | all-gather | bytes 819200 | tf_op jit(solution)/shard_map/all_gather | solution.py:92
  168.0 620.3 %reduce-scatter.4.cloned.1.call-done = f32[8,512]{1,0:T(8,128)} async-done(((f32[1024,512]{1,0:T(8,128)}), f32[8,512]{1,0:T(8,128)}) %reduce-scatter.4.cloned.1.call-update) | async-done | bytes 16400
  (119 shorter events, 47.7 us)
Async XLA Ops:
  8.1 6.5 collective-permute-start.1
  10.0 10.9 %collective-permute-start = (bf16[8,2,5120]{2,0,1:T(8,128)(2,1)S(1)}, bf16[8,2,5120]{2,0,1:T(8,128)(2,1)S(1)}, u32[]{:S(2)}, u32[]{:S(2)}) collective-permute-start(bf16[8,2,5120]{2,0,1:T(8,128)(2,1)S(1)} %copy.20), channel_id=1, source_target_pairs={{0,1},{1,2},{2,3},{4,5},{5,6},{6,7},{8,9},{9,10},{10,11},{12,13},{... | collective-permute-start | bytes 491528 | tf_op jit(solution)/shard_map/ppermute | solution.py:22
  29.2 4.7 collective-permute-start.3
  31.1 8.1 %collective-permute-start.2 = (bf16[8,2,5120]{2,0,1:T(8,128)(2,1)S(1)}, bf16[8,2,5120]{2,0,1:T(8,128)(2,1)S(1)}, u32[]{:S(2)}, u32[]{:S(2)}) collective-permute-start(bf16[8,2,5120]{2,0,1:T(8,128)(2,1)S(1)} %fusion.22), channel_id=1, source_target_pairs={{0,1},{1,2},{2,3},{4,5},{5,6},{6,7},{8,9},{9,10},{10,11},{12,13},{... | collective-permute-start | bytes 491528 | tf_op jit(solution)/shard_map/ppermute | solution.py:22
  44.4 2.3 copy-start
  47.9 4.7 collective-permute-start.5
  49.9 8.1 %collective-permute-start.4 = (bf16[8,2,5120]{2,0,1:T(8,128)(2,1)S(1)}, bf16[8,2,5120]{2,0,1:T(8,128)(2,1)S(1)}, u32[]{:S(2)}, u32[]{:S(2)}) collective-permute-start(bf16[8,2,5120]{2,0,1:T(8,128)(2,1)S(1)} %fusion.23), channel_id=1, source_target_pairs={{0,1},{1,2},{2,3},{4,5},{5,6},{6,7},{8,9},{9,10},{10,11},{12,13},{... | collective-permute-start | bytes 491528 | tf_op jit(solution)/shard_map/ppermute | solution.py:22
  66.6 4.7 collective-permute-start.7
  68.5 8.1 %collective-permute-start.6 = (bf16[8,2,5120]{2,0,1:T(8,128)(2,1)S(1)}, bf16[8,2,5120]{2,0,1:T(8,128)(2,1)S(1)}, u32[]{:S(2)}, u32[]{:S(2)}) collective-permute-start(bf16[8,2,5120]{2,0,1:T(8,128)(2,1)S(1)} %fusion.26), channel_id=1, source_target_pairs={{0,1},{1,2},{2,3},{4,5},{5,6},{6,7},{8,9},{9,10},{10,11},{12,13},{... | collective-permute-start | bytes 491528 | tf_op jit(solution)/shard_map/ppermute | solution.py:22
  85.3 24.9 %collective-permute-start.9 = (bf16[8,2,5120]{2,0,1:T(8,128)(2,1)S(1)}, bf16[8,2,5120]{2,0,1:T(8,128)(2,1)S(1)}, u32[]{:S(2)}, u32[]{:S(2)}) collective-permute-start(bf16[8,2,5120]{2,0,1:T(8,128)(2,1)S(1)} %fusion.29), channel_id=1, source_target_pairs={{1,0},{2,1},{3,2},{5,4},{6,5},{7,6},{9,8},{10,9},{11,10},{13,12},{... | collective-permute-start | bytes 491528 | tf_op jit(solution)/shard_map/ppermute | solution.py:24
  87.4 22.9 %collective-permute-start.8 = (bf16[8,2,5120]{2,0,1:T(8,128)(2,1)S(1)}, bf16[8,2,5120]{2,0,1:T(8,128)(2,1)S(1)}, u32[]{:S(2)}, u32[]{:S(2)}) collective-permute-start(bf16[8,2,5120]{2,0,1:T(8,128)(2,1)S(1)} %fusion.29), channel_id=1, source_target_pairs={{0,1},{1,2},{2,3},{4,5},{5,6},{6,7},{8,9},{9,10},{10,11},{12,13},{... | collective-permute-start | bytes 491528 | tf_op jit(solution)/shard_map/ppermute | solution.py:22
  91.0 38.1 %all-to-all-start = ((bf16[8,128,80]{2,0,1:T(8,128)(2,1)}), bf16[8,128,80]{2,0,1:T(8,128)(2,1)}, u32[]{:S(2)}, u32[]{:S(2)}) async-start(bf16[8,128,80]{2,0,1:T(8,128)(2,1)} %copy.26), calls=%async_computation | async-start | bytes 524288 | tf_op jit(solution)/shard_map/all_to_all | solution.py:87
  129.1 27.9 %all-to-all-start.1 = ((bf16[8,128,80]{2,0,1:T(8,128)(2,1)}), bf16[8,128,80]{2,0,1:T(8,128)(2,1)S(1)}, u32[]{:S(2)}, u32[]{:S(2)}) async-start(bf16[8,128,80]{2,0,1:T(8,128)(2,1)} %copy.29), calls=%async_computation.1 | async-start | bytes 524288 | tf_op jit(solution)/shard_map/all_to_all | solution.py:88
  138.2 650.0 %reduce-scatter.4.cloned.1.call-start = ((), (), s32[]{:S(2)}) async-start(), calls=%async_computation.3 | async-start | bytes 2113536
Sparse Core Ops, SparseCore 0:
  168.1 620.0 reduce-scatter.3
where the time goes:
time: 798 us; the launch traced here: 797 us
  waiting for transfers between devices  662 us (83%)
  starting transfers between devices  50.2 us (6%)
  local copies, waits for them, and re-layouts  33.8 us (4%)
  other arithmetic  17.8 us (2%)
  blocking collectives  17.4 us (2%)
  between operations  14.7 us (2%)
    unnamed x2, waiting for transfers between devices  620 us
    ppermute x5, waiting for transfers between devices, padded_2(): lax.ppermute(tail, axis, [(i, (i + 1) % count) for i in range(ends)])  22.1 us
    all_to_all x1, starting transfers between devices, per_device(): lax.all_to_all(filtered, 'band', split_axis=1, concat_axis=0, tiled=True)  19.2 us
  transfers between devices with their start and end apart: 13, of which 10 were waited for; matrix products, arithmetic and copies ran while one was open for 2% of the time, Pallas kernels for 0%

commit v1 on v0

--- a/solution.py
+++ b/solution.py
@@ -9,6 +9,12 @@
 DEGREE = 4
 filter_center = 5.5
 filter_radius = 4.5
+
+
+def stacked_exchange(x, axis, split, join):
+    cells = jnp.split(x, lax.axis_size(axis), axis=split)
+    received = lax.all_to_all(jnp.stack(cells), axis, 0, 0)
+    return jnp.concatenate(received, axis=join)
 
 
 def padded_2(cells, sides, width):
@@ -85,7 +91,7 @@
     applied = applied.reshape(orb_count, -1)
     cell_y, cell_h = (
         lax.all_to_all(filtered, "band", split_axis=1, concat_axis=0, tiled=True),
-        lax.all_to_all(applied, "band", split_axis=1, concat_axis=0, tiled=True),
+        stacked_exchange(applied, "band", 1, 0),
     )
     cell_y, cell_h = (
         lax.all_gather(cell_y, "domain", axis=1, tiled=True),

time: 798 us -> 876 us (1.098)
  local copies, waits for them, and re-layouts: 33.8 us -> 115 us
  waiting for transfers between devices: 662 us -> 652 us
    unnamed x8 -> x135, local copies, waits for them, and re-layouts: 4.38 us -> 86.2 us
    all_to_all x1, waiting for transfers between devices: 11 us -> 0.01 us  [per_device(): lax.all_to_all(filtered, 'band', split_axis=1, concat_axis=0, tiled=True)]
  transfers between devices with their start and end apart: 13 -> 13, of which waited for: 10 -> 9; matrix products, arithmetic and copies ran while one was open for 2% -> 11% of each run, Pallas kernels for 0% -> 0%
where the time goes in v1:
time: 876 us; the launch traced here: 875 us
  waiting for transfers between devices  652 us (74%)
  local copies, waits for them, and re-layouts  115 us (13%)
  starting transfers between devices  58 us (7%)
  other arithmetic  17.8 us (2%)
  blocking collectives  17.3 us (2%)
  between operations  14.8 us (2%)
    unnamed x2, waiting for transfers between devices  620 us
    unnamed x135, local copies, waits for them, and re-layouts  86.2 us
    ppermute x5, waiting for transfers between devices, padded_2(): lax.ppermute(tail, axis, [(i, (i + 1) % count) for i in range(ends)])  22.1 us
    all_to_all x1, starting transfers between devices, per_device(): lax.all_to_all(filtered, 'band', split_axis=1, concat_axis=0, tiled=True)  19.2 us
  transfers between devices with their start and end apart: 13, of which 9 were waited for; matrix products, arithmetic and copies ran while one was open for 11% of the time, Pallas kernels for 0%

profile of v1, /device:TPU:4, one launch (start us, length us, event | category | flops | bytes accessed | tf_op | source)
XLA Modules:
  0.0 875.5 jit_solution(1252765614496343046)
XLA Ops:
  8.1 1.9 collective-permute-start.1
  10.0 2.4 collective-permute-start
  14.7 6.3 collective-permute-done
  29.2 1.9 collective-permute-start.3
  31.1 2.4 collective-permute-start.2
  34.0 5.3 collective-permute-done.2
  44.4 2.0 fusion.5
  47.9 1.9 collective-permute-start.5
  49.9 2.4 collective-permute-start.4
  52.7 5.3 collective-permute-done.4
  63.2 2.0 fusion.9
  66.6 1.9 collective-permute-start.7
  68.5 2.6 collective-permute-start.6
  71.4 5.3 collective-permute-done.6
  81.8 2.0 fusion.13
  85.3 1.9 collective-permute-start.9
  87.4 2.4 collective-permute-start.8
  91.0 19.2 %all-to-all-start = ((bf16[8,128,80]{2,0,1:T(8,128)(2,1)}), bf16[8,128,80]{2,0,1:T(8,128)(2,1)}, u32[]{:S(2)}, u32[]{:S(2)}) async-start(bf16[8,128,80]{2,0,1:T(8,128)(2,1)} %copy.24), calls=%async_computation | async-start | bytes 524288 | tf_op jit(solution)/shard_map/all_to_all | solution.py:93
  199.3 16.9 %all-to-all-start.1 = ((bf16[128,8,80]{2,1,0:T(8,128)(2,1)}), bf16[128,8,80]{2,1,0:T(8,128)(2,1)S(1)}, u32[]{:S(2)}, u32[]{:S(2)}) async-start(bf16[128,8,80]{2,1,0:T(8,128)(2,1)} %constant_dynamic-update-slice_fusion), calls=%async_computation.1 | async-start | bytes 524288 | tf_op jit(solution)/shard_map/all_to_all | solution.py:16
  217.3 8.9 %all_gather.6 = bf16[1024,320]{0,1:T(8,128)(2,1)S(1)} all-gather(bf16[1024,80]{0,1:T(8,128)(2,1)S(1)} %copy.25), channel_id=1, replica_groups=mesh['band'=128,'domain'=4] {'domain'}, dimensions={1}, use_global_device_ids=true | all-gather | bytes 819200 | tf_op jit(solution)/shard_map/all_gather | solution.py:97
  226.8 8.2 all-to-all-done.1
  235.1 8.4 all_gather.7
  244.2 1.8 copy.29
  246.0 620.2 %reduce-scatter.4.cloned.1.call-done = f32[8,512]{1,0:T(8,128)} async-done(((f32[1024,512]{1,0:T(8,128)}), f32[8,512]{1,0:T(8,128)}) %reduce-scatter.4.cloned.1.call-update) | async-done | bytes 16400
  (244 shorter events, 127.0 us)
Async XLA Ops:
  8.1 6.5 collective-permute-start.1
  10.0 10.9 %collective-permute-start = (bf16[8,2,5120]{2,0,1:T(8,128)(2,1)S(1)}, bf16[8,2,5120]{2,0,1:T(8,128)(2,1)S(1)}, u32[]{:S(2)}, u32[]{:S(2)}) collective-permute-start(bf16[8,2,5120]{2,0,1:T(8,128)(2,1)S(1)} %copy.18), channel_id=1, source_target_pairs={{0,1},{1,2},{2,3},{4,5},{5,6},{6,7},{8,9},{9,10},{10,11},{12,13},{... | collective-permute-start | bytes 491528 | tf_op jit(solution)/shard_map/ppermute | solution.py:28
  29.2 4.7 collective-permute-start.3
  31.1 8.1 collective-permute-start.2
  44.4 2.3 copy-start
  47.9 4.7 collective-permute-start.5
  49.9 8.1 collective-permute-start.4
  66.6 4.7 collective-permute-start.7
  68.5 8.1 collective-permute-start.6
  85.3 24.9 %collective-permute-start.9 = (bf16[8,2,5120]{2,0,1:T(8,128)(2,1)S(1)}, bf16[8,2,5120]{2,0,1:T(8,128)(2,1)S(1)}, u32[]{:S(2)}, u32[]{:S(2)}) collective-permute-start(bf16[8,2,5120]{2,0,1:T(8,128)(2,1)S(1)} %fusion.29), channel_id=1, source_target_pairs={{1,0},{2,1},{3,2},{5,4},{6,5},{7,6},{9,8},{10,9},{11,10},{13,12},{... | collective-permute-start | bytes 491528 | tf_op jit(solution)/shard_map/ppermute | solution.py:30
  87.4 22.9 %collective-permute-start.8 = (bf16[8,2,5120]{2,0,1:T(8,128)(2,1)S(1)}, bf16[8,2,5120]{2,0,1:T(8,128)(2,1)S(1)}, u32[]{:S(2)}, u32[]{:S(2)}) collective-permute-start(bf16[8,2,5120]{2,0,1:T(8,128)(2,1)S(1)} %fusion.29), channel_id=1, source_target_pairs={{0,1},{1,2},{2,3},{4,5},{5,6},{6,7},{8,9},{9,10},{10,11},{12,13},{... | collective-permute-start | bytes 491528 | tf_op jit(solution)/shard_map/ppermute | solution.py:28
  91.0 108.3 %all-to-all-start = ((bf16[8,128,80]{2,0,1:T(8,128)(2,1)}), bf16[8,128,80]{2,0,1:T(8,128)(2,1)}, u32[]{:S(2)}, u32[]{:S(2)}) async-start(bf16[8,128,80]{2,0,1:T(8,128)(2,1)} %copy.24), calls=%async_computation | async-start | bytes 524288 | tf_op jit(solution)/shard_map/all_to_all | solution.py:93
  199.3 35.7 %all-to-all-start.1 = ((bf16[128,8,80]{2,1,0:T(8,128)(2,1)}), bf16[128,8,80]{2,1,0:T(8,128)(2,1)S(1)}, u32[]{:S(2)}, u32[]{:S(2)}) async-start(bf16[128,8,80]{2,1,0:T(8,128)(2,1)} %constant_dynamic-update-slice_fusion), calls=%async_computation.1 | async-start | bytes 524288 | tf_op jit(solution)/shard_map/all_to_all | solution.py:16
  216.2 650.1 %reduce-scatter.4.cloned.1.call-start = ((), (), s32[]{:S(2)}) async-start(), calls=%async_computation.3 | async-start | bytes 2113536
Sparse Core Ops, SparseCore 0:
  246.2 620.0 reduce-scatter.3
